TPU v7x, 128 devices: a whole 4x4x4 slice. The times are simulated.
128 devices in a mesh: split: 16 (over x, y_hi, core), shard: 8 (over y_lo, z).
Axes of the slice: x: 4, y: 4 (y_hi: 2, y_lo: 2; y = y_hi * 2 + y_lo), z: 4, core: 2. Of those that a mesh axis runs over, the one named last changes fastest.
Arguments:
- strain: bfloat16 [3, 4096], P(None, ('split', 'shard')), may hold values from -6 to 6
- basis: bfloat16 [16, 400, 2048], P('split', 'shard'), may hold values from -0.125 to 0.125
- recon: bfloat16 [16, 2, 4096, 400], P('split', None, 'shard'), may hold values from -0.3125 to 0.3125
Outputs:
- snr2: float32 [16, 4096, 2048], P('split', 'shard')
- loudest: float32 [2048], replicated
All inputs are finite; a program needn't handle non-finite values.
Results may differ from a plain program's by a relative error of at most 0.0025.
Values may be sent and summed in bfloat16 or wider, within the bound.
No kernel may reach another device: no remote copies, remote signals or barrier semaphores. Data moves between devices by JAX's collectives and lax.ppermute only.
A program may use at most 128 MiB of HBM per device.

v0:
```python
import jax
import jax.numpy as jnp
from jax import lax
from jax.sharding import PartitionSpec as P


def toeplitz_block(segment, rows, cols):
    width = rows + cols - 1
    turned = jnp.concatenate([segment[rows - 1 :], segment[: rows - 1]])
    flat = jnp.broadcast_to(turned, (rows, width)).reshape(-1)[: rows * (width - 1)]
    return flat.reshape(rows, width - 1)[:, :cols]


def filter_series(signal, filters):
    taps = filters.shape[1]
    tout = signal.shape[0] - taps
    tblock = min(512, tout)
    kblock = min(512, taps)
    outputs = []
    for tpos in range(tout // tblock):
        pieces = []
        for kpos in range(taps // kblock):
            begin = tpos * tblock + taps - (kpos + 1) * kblock
            segment = signal[begin : begin + kblock + tblock - 1]
            pieces.append(toeplitz_block(segment, kblock, tblock))
        frame = jnp.concatenate(pieces, axis=0)
        outputs.append(jnp.dot(filters, frame, preferred_element_type=jnp.float32))
    return jnp.concatenate(outputs, axis=1)


def all_detectors(whole, filters):
    return jnp.stack(
        [filter_series(whole[det], filters).astype(jnp.bfloat16) for det in range(whole.shape[0])]
    )


def per_device(strain, basis, recon):
    whole = lax.all_gather(strain, ("split", "shard"), axis=1, tiled=True)
    filters = basis[0]
    own_series = all_detectors(whole, filters)
    series = lax.all_gather(own_series, "shard", axis=1, tiled=True)
    weights = recon[0]
    detectors = series.shape[0]
    scale = 1.0 / (2.0 * detectors)
    templ = weights.shape[1]
    mblock = min(256, templ)
    blocks = []
    for mpos in range(templ // mblock):
        part = weights[:, mpos * mblock : (mpos + 1) * mblock]
        total = jnp.zeros((mblock, series.shape[2]), jnp.float32)
        for det in range(detectors):
            zvals = jnp.einsum("qml,lt->qmt", part, series[det], preferred_element_type=jnp.float32)
            total = total + jnp.sum(zvals * zvals, axis=0)
        blocks.append(total * scale)
    snr_local = jnp.concatenate(blocks, axis=0)
    loudest = lax.pmax(jnp.max(snr_local, axis=0), ("split", "shard"))
    return (snr_local[None], loudest)


def solution(mesh):
    return jax.shard_map(
        per_device,
        mesh=mesh,
        in_specs=(
            P(None, ("split", "shard")),
            P("split", "shard", None),
            P("split", None, "shard", None),
        ),
        out_specs=(P("split", "shard", None), P()),
        check_vma=False,
    )
```

profile of v0, /device:TPU:1, one launch (start us, length us, event | category | flops | bytes accessed | tf_op | source)
XLA Modules:
  0.0 618.8 jit_solution(15885630971313744312)
XLA Ops:
  7.2 303.4 %all-gather = bf16[128,32,3]{1,2,0:T(4,128)(2,1)S(1)} all-gather(bf16[1,32,3]{1,2,0:T(4,128)(2,1)} %bitcast.105), channel_id=1, replica_groups=mesh['split'=16,'shard'=8] {'split','shard'}, dimensions={0}, use_global_device_ids=true | all-gather | bytes 24768 | tf_op jit(solution)/shard_map/all_gather | solution.py:38
  313.6 1.7 reshape.428
  315.4 1.8 reshape.429
  318.2 1.7 reshape.432
  319.9 1.8 reshape.433
  322.8 1.7 reshape.434
  324.5 1.8 reshape.435
  327.3 2.0 reshape.436
  329.4 1.8 reshape.437
  331.4 1.7 reshape.438
  333.1 1.8 reshape.439
  335.9 1.7 reshape.440
  337.7 1.8 reshape.441
  340.5 1.7 reshape.442
  342.2 1.8 reshape.443
  345.0 1.8 reshape.444
  346.9 1.8 reshape.445
  348.9 1.7 reshape.446
  350.7 1.8 reshape.447
  352.6 1.9 fusion.144
  355.1 1.7 reshape.448
  356.9 1.8 reshape.449
  358.8 1.7 fusion.150
  360.7 1.9 reshape.450
  362.6 1.8 reshape.451
  364.5 2.2 fusion.153
  366.8 1.7 reshape.452
  368.6 1.8 reshape.453
  371.4 1.7 reshape.454
  373.2 1.8 reshape.455
  376.0 1.7 reshape.456
  377.7 1.8 reshape.457
  381.0 1.7 reshape.458
  382.8 1.8 reshape.459
  384.8 1.7 reshape.460
  386.5 1.8 reshape.461
  388.5 2.5 fusion.156
  391.0 1.1 fusion.159
  392.2 1.7 reshape.462
  394.0 1.8 reshape.463
  395.9 2.3 fusion.162
  398.3 1.8 reshape.464
  400.3 1.8 reshape.465
  402.2 2.1 fusion.165
  404.4 1.7 reshape.430
  406.2 1.8 reshape.431
  409.1 1.7 reshape.424
  410.9 1.8 reshape.425
  413.7 1.7 reshape.426
  415.5 1.8 reshape.427
  417.4 1.8 fusion.141
  422.3 1.4 copy.7
  423.7 84.6 %all-gather.3.cloned.1.call-done = bf16[3,400,2048]{2,0,1:T(4,128)(2,1)} async-done(((bf16[3,50,2048]{2,0,1:T(4,128)(2,1)}), bf16[3,400,2048]{2,0,1:T(4,128)(2,1)}) %all-gather.3.cloned.1.call-update) | async-done | bytes 4915216 | tf_op jit(solution)/shard_map/all_gather | solution.py:41
  508.3 15.7 %fusion.202 = (bf16[1,400,2048]{2,0,1:T(2,128)(2,1)S(1)}, bf16[1,400,2048]{2,0,1:T(2,128)(2,1)S(1)}, bf16[1,400,2048]{2,0,1:T(2,128)(2,1)S(1)}) fusion(bf16[3,400,2048]{2,0,1:T(4,128)(2,1)} %all-gather.3.cloned.1.call-done), kind=kLoop, calls=%fused_computation.230 | loop fusion | bytes 9830400 | tf_op jit(solution)/shard_map/slice | solution.py:52
  524.0 2.0 multiply_reduce_fusion.1
  526.0 2.0 multiply_reduce_fusion.4
  528.0 2.0 multiply_reduce_fusion.2
  530.0 2.0 multiply_reduce_fusion.5
  532.0 2.0 multiply_reduce_fusion
  534.0 2.0 multiply_reduce_fusion.3
  536.0 1.9 fusion.198
  537.9 64.2 %pmax.7 = f32[2048]{0:T(1024)} all-reduce(f32[2048]{0:T(1024)S(1)} %reduce_max.19), channel_id=1, replica_groups=mesh['split'=16,'shard'=8] {'split','shard'}, use_global_device_ids=true, to_apply=%region_8.9 | all-reduce | flops 2048 | bytes 16384 | tf_op jit(solution)/shard_map/pmax | solution.py:56
  602.1 4.1 maximum_bitcast_fusion
  606.2 5.3 copy.11
  (196 shorter events, 20.8 us)
Async XLA Ops:
  7.2 345.4 %copy-start = (bf16[1,50,2048]{2,1,0:T(8,128)(2,1)S(1)}, bf16[1,50,2048]{2,1,0:T(8,128)(2,1)}, u32[]{:S(2)}) copy-start(bf16[1,50,2048]{2,1,0:T(8,128)(2,1)} %param.4) | copy-start | bytes 614404
  7.2 501.1 %all-gather.3.cloned.1.call-start = ((), (), s32[]{:S(2)}) async-start(), calls=%async_computation | async-start | bytes 7372800 | tf_op jit(solution)/shard_map/all_gather | solution.py:41
  331.2 1.8 copy-start.1
  348.8 1.8 copy-start.2
  350.7 1.9 slice-start.1
  350.7 1.9 copy-start.8
  352.6 1.9 copy-start.12
  352.6 1.9 copy-start.10
  352.6 1.9 copy-start.16
  358.8 1.7 copy-start.19
  358.8 1.7 copy-start.39
  358.8 1.7 copy-start.41
  362.5 2.0 copy-start.13
  364.5 2.2 copy-start.37
  364.5 2.2 copy-start.40
  368.5 2.8 copy-start.35
  368.5 2.8 copy-start.38
  373.1 2.8 copy-start.33
  373.1 2.7 copy-start.36
  377.6 2.8 copy-start.31
  377.7 2.8 copy-start.34
  382.7 1.9 copy-start.29
  382.8 1.9 copy-start.32
  384.6 1.8 copy-start.3
  386.5 1.9 slice-start.2
  386.5 1.9 copy-start.9
  388.4 2.5 copy-start.14
  388.5 2.5 copy-start.11
  388.5 2.5 copy-start.17
  391.0 1.1 copy-start.27
  391.0 1.1 copy-start.30
  395.8 2.3 copy-start.20
  395.9 2.3 copy-start.28
  400.2 2.0 copy-start.15
  402.1 2.2 copy-start.26
  406.1 1.9 copy-start.44
  406.1 1.9 copy-start.45
  408.0 1.0 copy-start.4
  410.8 2.8 copy-start.42
  410.8 2.8 copy-start.43
  415.4 2.0 slice-start
  415.4 2.0 copy-start.6
  417.4 1.8 copy-start.7
  417.4 1.8 copy-start.18
  419.2 1.0 copy-start.5
  420.2 1.0 slice-start.3
  421.2 0.8 copy-start.21
  421.2 0.8 copy-start.22
  421.2 0.9 copy-start.23
  421.3 0.9 copy-start.24
  421.3 0.9 copy-start.25
  423.7 100.3 %copy-start.46 = (bf16[1,2,512,400]{2,3,1,0:T(8,128)(2,1)S(1)}, bf16[1,2,512,400]{2,3,1,0:T(8,128)(2,1)}, u32[]{:S(2)}) copy-start(bf16[1,2,512,400]{2,3,1,0:T(8,128)(2,1)} %param.5) | copy-start | bytes 2457604
Sparse Core Ops, SparseCore 0:
  423.8 84.4 all-gather.2
where the time goes:
time: 628 us; the launch traced here: 619 us
  blocking collectives  368 us (59%)
  local copies, waits for them, and re-layouts  115 us (18%)
  waiting for transfers between devices  84.6 us (13%)
  matrix products  29.4 us (5%)
  between operations  15.9 us (3%)
  other arithmetic  6.67 us (1%)
    all_gather x1, blocking collectives, per_device(): whole = lax.all_gather(strain, ('split', 'shard'), axis=1, tiled=True)  303 us
    all_gather x1, waiting for transfers between devices, per_device(): series = lax.all_gather(own_series, 'shard', axis=1, tiled=True)  84.6 us
    pmax x1, blocking collectives, per_device(): loudest = lax.pmax(jnp.max(snr_local, axis=0), ('split', 'shard'))  64.2 us
    reshape x21, local copies, waits for them, and re-layouts, toeplitz_block(): return flat.reshape(rows, width - 1)[:, :cols]  38.2 us
    reshape x21, local copies, waits for them, and re-layouts, toeplitz_block(): jnp.broadcast_to(turned, (rows, width)).reshape(-1)[:rows * (width - 1)]  35.8 us
    dot_general x12, matrix products, filter_series(): outputs.append(jnp.dot(filters, frame, preferred_element_type=jnp.float32))  17.4 us
    slice x1, local copies, waits for them, and re-layouts, per_device(): series[det]  15.7 us
  transfers between devices with their start and end apart: 1, of which 1 were waited for; matrix products, arithmetic and copies ran while one was open for 0% of the time, Pallas kernels for 0%

commit v1 on v0

--- a/solution.py
+++ b/solution.py
@@ -38,7 +38,9 @@
     whole = lax.all_gather(strain, ("split", "shard"), axis=1, tiled=True)
     filters = basis[0]
     own_series = all_detectors(whole, filters)
-    series = lax.all_gather(own_series, "shard", axis=1, tiled=True)
+    series = jnp.concatenate(
+        lax.all_to_all(jnp.stack([own_series] * lax.axis_size("shard")), "shard", 0, 0), axis=1
+    )
     weights = recon[0]
     detectors = series.shape[0]
     scale = 1.0 / (2.0 * detectors)

time: 628 us -> 595 us (0.947)
  waiting for transfers between devices: 84.6 us -> 0 us
  blocking collectives: 368 us -> 432 us
  between operations: 15.9 us -> 2.46 us
    all_gather x1 -> x0, waiting for transfers between devices: 84.6 us -> none  [per_device(): series = lax.all_gather(own_series, 'shard', axis=1, tiled=True)]
    all_to_all x0 -> x1, blocking collectives: none -> 48.5 us  [per_device(): lax.all_to_all(jnp.stack([own_series] * lax.axis_size('shard')), 'shard',...]
    pmax x1, blocking collectives: 64.2 us -> 80.1 us  [per_device(): loudest = lax.pmax(jnp.max(snr_local, axis=0), ('split', 'shard'))]
    slice x1, local copies, waits for them, and re-layouts: 15.7 us -> 2.46 us  [per_device(): series[det]]
    squeeze x0 -> x3, local copies, waits for them, and re-layouts: none -> 6.63 us  [per_device(): series[det]]
  transfers between devices with their start and end apart: 1 -> 0, of which waited for: 1 -> 0; matrix products, arithmetic and copies ran while one was open for 0% -> 0% of each run, Pallas kernels for 0% -> 0%
where the time goes in v1:
time: 595 us; the launch traced here: 586 us
  blocking collectives  432 us (73%)
  local copies, waits for them, and re-layouts  110 us (18%)
  matrix products  35.5 us (6%)
  other arithmetic  6.61 us (1%)
    all_gather x1, blocking collectives, per_device(): whole = lax.all_gather(strain, ('split', 'shard'), axis=1, tiled=True)  303 us
    pmax x1, blocking collectives, per_device(): loudest = lax.pmax(jnp.max(snr_local, axis=0), ('split', 'shard'))  80.1 us
    all_to_all x1, blocking collectives, per_device(): lax.all_to_all(jnp.stack([own_series] * lax.axis_size('shard')), 'shard',...  48.5 us
    reshape x21, local copies, waits for them, and re-layouts, toeplitz_block(): return flat.reshape(rows, width - 1)[:, :cols]  38.4 us
    reshape x21, local copies, waits for them, and re-layouts, toeplitz_block(): jnp.broadcast_to(turned, (rows, width)).reshape(-1)[:rows * (width - 1)]  35.8 us
    dot_general x6, matrix products, per_device(): jnp.einsum('qml,lt->qmt', part, series[det], preferred_element_type=jnp.f...  18.1 us
    dot_general x12, matrix products, filter_series(): outputs.append(jnp.dot(filters, frame, preferred_element_type=jnp.float32))  17.4 us

profile of v1, /device:TPU:1, one launch (start us, length us, event | category | flops | bytes accessed | tf_op | source)
XLA Modules:
  0.0 586.2 jit_solution(10999948318656270127)
XLA Ops:
  0.6 303.4 %all-gather = bf16[128,32,3]{1,2,0:T(4,128)(2,1)S(1)} all-gather(bf16[1,32,3]{1,2,0:T(4,128)(2,1)} %bitcast.104), channel_id=1, replica_groups=mesh['split'=16,'shard'=8] {'split','shard'}, dimensions={0}, use_global_device_ids=true | all-gather | bytes 24768 | tf_op jit(solution)/shard_map/all_gather | solution.py:38
  307.1 1.7 reshape.440
  308.8 1.8 reshape.441
  311.6 1.7 reshape.444
  313.4 1.8 reshape.445
  316.2 1.7 reshape.446
  317.9 1.8 reshape.447
  320.7 2.0 reshape.448
  322.8 1.8 reshape.449
  324.8 1.7 reshape.450
  326.5 1.8 reshape.451
  329.3 1.7 reshape.452
  331.1 1.8 reshape.453
  333.9 1.7 reshape.454
  335.6 1.8 reshape.455
  338.4 1.8 reshape.456
  340.3 1.8 reshape.457
  342.3 1.7 reshape.458
  344.1 1.8 reshape.459
  346.0 1.9 fusion.144
  348.6 1.7 reshape.460
  350.3 1.8 reshape.461
  352.2 1.7 fusion.150
  354.1 1.9 reshape.462
  356.1 1.8 reshape.463
  358.0 2.2 fusion.153
  360.3 1.7 reshape.464
  362.0 1.8 reshape.465
  364.8 1.7 reshape.466
  366.6 1.8 reshape.467
  369.4 1.7 reshape.468
  371.2 1.8 reshape.469
  374.4 1.7 reshape.470
  376.1 1.8 reshape.471
  378.1 1.7 reshape.472
  379.9 1.8 reshape.473
  381.8 2.5 fusion.156
  385.6 1.7 reshape.474
  387.3 1.8 reshape.475
  389.2 2.3 fusion.162
  391.7 1.8 reshape.476
  393.6 1.8 reshape.477
  395.5 2.1 fusion.165
  397.8 1.7 reshape.442
  399.5 1.8 reshape.443
  402.5 1.7 reshape.436
  404.2 1.8 reshape.437
  407.1 1.7 reshape.438
  408.8 2.0 reshape.439
  410.9 1.8 fusion.141
  416.6 48.5 %all_to_all.5 = bf16[8,3,50,2048]{3,2,1,0:T(8,128)(2,1)S(1)} all-to-all(bf16[8,3,50,2048]{3,2,1,0:T(8,128)(2,1)S(1)} %stack.5), channel_id=1, replica_groups=mesh['split'=16,'shard'=8] {'shard'}, dimensions={0} | all-to-all | bytes 9830400 | tf_op jit(solution)/shard_map/all_to_all | solution.py:42
  465.0 2.5 fusion.202
  467.5 2.7 reshape.481
  470.2 4.3 multiply_reduce_fusion.2
  474.5 2.6 multiply_reduce_fusion.5
  477.1 2.6 reshape.483
  479.7 4.3 multiply_reduce_fusion
  483.9 2.6 multiply_reduce_fusion.3
  486.6 1.4 reshape.482
  488.0 3.0 multiply_reduce_fusion.1
  494.4 1.9 fusion.198
  496.3 80.1 %pmax.7 = f32[2048]{0:T(1024)} all-reduce(f32[2048]{0:T(1024)S(1)} %reduce_max.19), channel_id=1, replica_groups=mesh['split'=16,'shard'=8] {'split','shard'}, use_global_device_ids=true, to_apply=%region_8.9 | all-reduce | flops 2048 | bytes 16384 | tf_op jit(solution)/shard_map/pmax | solution.py:58
  576.4 4.1 maximum_bitcast_fusion
  580.5 5.3 copy.7
  (211 shorter events, 26.0 us)
Async XLA Ops:
  0.6 345.3 %copy-start = (bf16[1,50,2048]{2,1,0:T(8,128)(2,1)S(1)}, bf16[1,50,2048]{2,1,0:T(8,128)(2,1)}, u32[]{:S(2)}) copy-start(bf16[1,50,2048]{2,1,0:T(8,128)(2,1)} %param.4) | copy-start | bytes 614404
  324.6 1.8 copy-start.1
  342.2 1.8 copy-start.2
  344.1 1.9 slice-start.1
  344.1 1.9 copy-start.15
  346.0 1.9 copy-start.19
  346.0 1.9 copy-start.17
  346.0 1.9 copy-start.23
  352.2 1.7 copy-start.26
  352.2 1.7 copy-start.46
  352.2 1.7 copy-start.48
  356.0 2.0 copy-start.20
  357.9 2.2 copy-start.44
  357.9 2.2 copy-start.47
  361.9 2.8 copy-start.42
  361.9 2.8 copy-start.45
  366.5 2.8 copy-start.40
  366.5 2.7 copy-start.43
  371.1 2.8 copy-start.38
  371.1 2.8 copy-start.41
  376.1 1.9 copy-start.36
  376.1 1.9 copy-start.39
  378.0 1.8 copy-start.3
  379.9 1.9 slice-start.2
  379.9 1.9 copy-start.16
  381.8 2.5 copy-start.21
  381.8 2.5 copy-start.18
  381.8 2.5 copy-start.24
  384.3 1.1 copy-start.34
  384.3 1.1 copy-start.37
  389.2 2.3 copy-start.27
  389.2 2.3 copy-start.35
  393.5 2.0 copy-start.22
  395.5 2.2 copy-start.33
  399.5 1.9 copy-start.51
  399.5 1.9 copy-start.52
  401.4 1.0 copy-start.4
  404.1 2.8 copy-start.49
  404.1 2.8 copy-start.50
  408.7 2.2 slice-start
  408.7 2.2 copy-start.13
  410.9 1.8 copy-start.14
  410.9 1.8 copy-start.25
  412.7 1.0 copy-start.12
  413.8 1.0 slice-start.3
  414.8 0.8 copy-start.28
  414.8 0.8 copy-start.29
  414.8 0.9 copy-start.30
  414.8 0.9 copy-start.31
  414.8 0.9 copy-start.32
  467.5 2.7 copy-start.53
  470.2 4.3 copy-start.9
  479.7 4.3 copy-start.10
  488.0 3.0 copy-start.11
  491.0 1.6 copy-start.5
  491.0 2.2 copy-start.6
  491.0 2.8 copy-start.7
  491.0 3.4 copy-start.8
